TPU v7x, 32 devices: a whole 2x2x4 slice. The times are simulated.
32 devices in a mesh: sample: 4 (over y, x), fsdp: 8 (over z, core).
Axes of the slice: x: 2, y: 2, z: 4, core: 2. Of those that a mesh axis runs over, the one named last changes fastest.
Arguments:
- seed_step: int32 [2], replicated, may hold values from 0 to 16777215
- attn: bfloat16 [16384, 2048], P(('sample', 'fsdp')), may hold values from -6 to 6
- resid: bfloat16 [16384, 4096], P(('sample', 'fsdp')), may hold values from -36 to 36
- cotangent: bfloat16 [16384, 4096], P(('sample', 'fsdp')), may hold values from -6 to 6
- gain: bfloat16 [4096], replicated, may hold values from 0.099609375 to 1.8984375
- mean: float32 [2048, 4096], P('fsdp'), may hold values from -6 to 6
- hess: float32 [2048, 4096], P('fsdp'), may hold values from 0.25 to 4
- momentum: float32 [2048, 4096], P('fsdp'), may hold values from -3 to 3
Outputs:
- new_mean: float32 [2048, 4096], P('fsdp')
- new_hess: float32 [2048, 4096], P('fsdp')
- new_momentum: float32 [2048, 4096], P('fsdp')
All inputs are finite; a program needn't handle non-finite values.
Results may differ from a plain program's by a relative error of at most 0.0035.
Values may be sent and summed in bfloat16 or wider, within the bound.
A program may use at most 192 MiB of HBM per device.

v0:
```python
import jax
import jax.numpy as jnp
from jax import lax
from jax.experimental.layout import Layout, with_layout_constraint
from jax.sharding import PartitionSpec as P

ess_value = 10.0
decay_first = 0.8
decay_second = 0.8
step_size = 0.3
damping = 0.1
norm_eps = 1e-05


def noise_table(seed_step, group_id, row_start, row_count, in_width, width, col_start, col_count):
    row_index = jnp.arange(row_count, dtype=jnp.int32)[:, None] + row_start
    col_index = jnp.arange(col_count, dtype=jnp.int32)[None, :] + col_start
    mixing = (group_id * in_width + row_index) * width + col_index
    mixing = jnp.bitwise_xor(mixing, seed_step[0])
    mixing = mixing * 668265261 + seed_step[1] * 374761393
    mixing = jnp.bitwise_xor(mixing, jnp.right_shift(mixing, 15) & 131071)
    mixing = mixing * 739982445
    mixing = jnp.bitwise_xor(mixing, jnp.right_shift(mixing, 12) & 1048575)
    mixing = mixing * 695872825
    mixing = jnp.bitwise_xor(mixing, jnp.right_shift(mixing, 15) & 131071)
    first_unif = ((mixing & 4095).astype(jnp.float32) + 0.5) / 4096.0
    second_unif = ((jnp.right_shift(mixing, 12) & 4095).astype(jnp.float32) + 0.5) / 4096.0
    return 2.449489742783178 * (first_unif + second_unif - 1.0)


def ivon_update(mean, hess, momentum, grad_sum, curv_sum, groups):
    grad_mean = grad_sum / groups
    hess_est = curv_sum / groups
    new_momentum = decay_first * momentum + (1.0 - decay_first) * grad_mean
    new_hess = (
        decay_second * hess
        + (1.0 - decay_second) * hess_est
        + 0.5 * (1.0 - decay_second) ** 2 * (hess - hess_est) ** 2 / (hess + damping)
    )
    new_mean = mean - step_size * (new_momentum + damping * mean) / (new_hess + damping)
    return (new_mean, new_hess, new_momentum)


def row_major(value):
    return with_layout_constraint(value, Layout(major_to_minor=(0, 1)))


CHUNKS = 4


def per_device(seed_step, attn, resid, cotangent, gain, mean, hess, momentum):
    own_rows = mean.shape[0]
    width = mean.shape[1]
    in_width = attn.shape[1]
    scaling = in_width ** (-0.5)
    groups = lax.axis_size("sample")
    group_id = lax.axis_index("sample")
    shard_id = lax.axis_index("fsdp")
    part = width // CHUNKS
    cuts = [slice(c * part, (c + 1) * part) for c in range(CHUNKS)]
    epsilons, gathered = ([], [])
    for c, cut in enumerate(cuts):
        sigma = 1.0 / jnp.sqrt(ess_value * (hess[:, cut] + damping))
        epsilon = noise_table(
            seed_step, group_id, shard_id * own_rows, own_rows, in_width, width, c * part, part
        )
        sampled = (
            mean[:, cut].astype(jnp.bfloat16).astype(jnp.float32)
            + sigma.astype(jnp.bfloat16).astype(jnp.float32) * epsilon
        ).astype(jnp.bfloat16)
        epsilons.append(epsilon / sigma)
        gathered.append(lax.all_gather(row_major(sampled), "fsdp", axis=0, tiled=True))
    totals = []
    square = jnp.zeros((attn.shape[0], 1), jnp.float32)
    cross = jnp.zeros((attn.shape[0], 1), jnp.float32)
    for c, cut in enumerate(cuts):
        product = row_major(
            jnp.dot(attn, row_major(gathered[c]), preferred_element_type=jnp.float32)
        )
        total = resid[:, cut].astype(jnp.float32) + product * scaling
        upstream = gain[cut].astype(jnp.float32)[None, :] * cotangent[:, cut].astype(jnp.float32)
        square = square + jnp.sum(total * total, axis=-1, keepdims=True)
        cross = cross + jnp.sum(total * upstream, axis=-1, keepdims=True)
        totals.append(total)
    inverse = lax.rsqrt(square / width + norm_eps)
    slope = inverse**3 * (cross / width)
    sums = []
    for c, cut in enumerate(cuts):
        upstream = gain[cut].astype(jnp.float32)[None, :] * cotangent[:, cut].astype(jnp.float32)
        back_low = (inverse * upstream - totals[c] * slope).astype(jnp.bfloat16)
        grad = lax.psum_scatter(
            row_major(
                (
                    lax.dot_general(
                        attn,
                        row_major(back_low),
                        (((0,), (0,)), ((), ())),
                        preferred_element_type=jnp.float32,
                    )
                    * scaling
                ).astype(jnp.bfloat16)
            ),
            "fsdp",
            scatter_dimension=0,
            tiled=True,
        )
        if sums:
            grad, sums[-1] = lax.optimization_barrier((grad, sums[-1]))
        grad = row_major(grad)
        curvature = (grad.astype(jnp.float32) * epsilons[c]).astype(jnp.bfloat16)
        sums.append(lax.psum((grad, row_major(curvature)), "sample"))
    grad_sum = jnp.concatenate([s[0] for s in sums], axis=1).astype(jnp.float32)
    curv_sum = jnp.concatenate([s[1] for s in sums], axis=1).astype(jnp.float32)
    return ivon_update(mean, hess, momentum, grad_sum, curv_sum, groups)


def solution(mesh):
    placed = (
        P(),
        P(("sample", "fsdp"), None),
        P(("sample", "fsdp"), None),
        P(("sample", "fsdp"), None),
        P(),
        P("fsdp", None),
        P("fsdp", None),
        P("fsdp", None),
    )
    return jax.shard_map(
        per_device,
        mesh=mesh,
        in_specs=placed,
        out_specs=(P("fsdp", None), P("fsdp", None), P("fsdp", None)),
        check_vma=False,
    )
```

profile of v0, /device:TPU:0, one launch (start us, length us, event | category | flops | bytes accessed | tf_op | source)
XLA Modules:
  0.0 671.1 jit_solution(17493066383043819291)
XLA Ops:
  13.1 7.5 %add_convert_fusion.1 = (bf16[256,1024]{1,0:T(8,128)(2,1)}, bf16[256,1024]{1,0:T(8,128)(2,1)}, bf16[256,1024]{1,0:T(8,128)(2,1)}, bf16[256,1024]{1,0:T(8,128)(2,1)}) fusion(f32[256,4096]{1,0:T(8,128)} %param.14, bf16[256,4096]{1,0:T(8,128)(2,1)} %convert.6, s32[]{:T(128)} %bitcast.1, s32[]{:T(128)} %bitcast, s32[1024]{0:T(1024)S(1)} %get-tuple-element.54, ...), kind=kLoop, calls=%fused_computation.61 | loop fusion | flops 35651584 | bytes 8401928 | tf_op jit(solution)/shard_map/convert_element_type | solution.py:70
  22.9 47.7 %all-gather.9.cloned.1.call-done = bf16[2048,1024]{1,0:T(8,128)(2,1)} async-done(((bf16[256,1024]{1,0:T(8,128)(2,1)}), bf16[2048,1024]{1,0:T(8,128)(2,1)}) %all-gather.9.cloned.1.call-update) | async-done | bytes 4194320 | tf_op jit(solution)/shard_map/all_gather | solution.py:72
  70.6 6.2 fusion.11
  76.8 41.9 %all-gather.5.cloned.1.call-done = bf16[2048,1024]{1,0:T(8,128)(2,1)} async-done(((bf16[256,1024]{1,0:T(8,128)(2,1)}), bf16[2048,1024]{1,0:T(8,128)(2,1)}) %all-gather.5.cloned.1.call-update) | async-done | bytes 4194320 | tf_op jit(solution)/shard_map/all_gather | solution.py:72
  118.7 6.1 fusion.13
  124.8 41.4 %all-gather.11.cloned.1.call-done = bf16[2048,1024]{1,0:T(8,128)(2,1)} async-done(((bf16[256,1024]{1,0:T(8,128)(2,1)}), bf16[2048,1024]{1,0:T(8,128)(2,1)}) %all-gather.11.cloned.1.call-update) | async-done | bytes 4194320 | tf_op jit(solution)/shard_map/all_gather | solution.py:72
  166.2 6.1 fusion.10
  172.3 41.2 %all-gather.7.cloned.1.call-done = bf16[2048,1024]{1,0:T(8,128)(2,1)} async-done(((bf16[256,1024]{1,0:T(8,128)(2,1)}), bf16[2048,1024]{1,0:T(8,128)(2,1)}) %all-gather.7.cloned.1.call-update) | async-done | bytes 4194320 | tf_op jit(solution)/shard_map/all_gather | solution.py:72
  213.6 9.8 %multiply_reduce_fusion.2 = (f32[512]{0:T(512)S(1)}, f32[512]{0:T(512)S(1)}, f32[512]{0:T(512)S(1)}, f32[512]{0:T(512)S(1)}, f32[512]{0:T(512)S(1)}, /*index=5*/...) fusion(f32[1024]{0:T(1024)S(1)} %get-tuple-element.48, bf16[512,4096]{1,0:T(8,128)(2,1)} %param.11, ...), kind=kOutput, calls=%fused_computation.34 | convolution fusion | flops 2161635328 | bytes 19955712 | tf_op jit(solution)/shard_map/dot_general | solution.py:78
  223.4 5.9 fusion.7
  229.6 6.4 fusion.6
  236.1 42.1 %reduce-scatter.7.cloned.1.call-done = bf16[256,1024]{1,0:T(8,128)(2,1)} async-done(((bf16[2048,1024]{1,0:T(8,128)(2,1)}), bf16[256,1024]{1,0:T(8,128)(2,1)}) %reduce-scatter.7.cloned.1.call-update) | async-done | bytes 524304 | tf_op jit(solution)/shard_map/reduce_scatter | solution.py:91
  278.2 3.9 multiply_convert_fusion.7
  282.2 6.4 fusion.8
  288.7 40.4 %reduce-scatter.5.cloned.1.call-done = bf16[256,1024]{1,0:T(8,128)(2,1)} async-done(((bf16[2048,1024]{1,0:T(8,128)(2,1)}), bf16[256,1024]{1,0:T(8,128)(2,1)}) %reduce-scatter.5.cloned.1.call-update) | async-done | bytes 524304 | tf_op jit(solution)/shard_map/reduce_scatter | solution.py:91
  329.1 53.9 %all-reduce.15.cloned.1.call-done = (bf16[256,1024]{1,0:T(8,128)(2,1)}, bf16[256,1024]{1,0:T(8,128)(2,1)}) async-done(((bf16[256,1024]{1,0:T(8,128)(2,1)}, bf16[256,1024]{1,0:T(8,128)(2,1)}), (bf16[256,1024]{1,0:T(8,128)(2,1)}, bf16[256,1024]{1,0:T(8,128)(2,1)})) %all-reduce.15.cloned.1.call-update) | async-done | bytes 1048592 | tf_op jit(solution)/shard_map/psum | solution.py:111
  383.0 3.9 multiply_convert_fusion.6
  386.9 6.4 fusion.9
  393.5 42.5 %reduce-scatter.9.cloned.1.call-done = bf16[256,1024]{1,0:T(8,128)(2,1)} async-done(((bf16[2048,1024]{1,0:T(8,128)(2,1)}), bf16[256,1024]{1,0:T(8,128)(2,1)}) %reduce-scatter.9.cloned.1.call-update) | async-done | bytes 524304 | tf_op jit(solution)/shard_map/reduce_scatter | solution.py:91
  435.9 53.9 %all-reduce.13.cloned.1.call-done = (bf16[256,1024]{1,0:T(8,128)(2,1)}, bf16[256,1024]{1,0:T(8,128)(2,1)}) async-done(((bf16[256,1024]{1,0:T(8,128)(2,1)}, bf16[256,1024]{1,0:T(8,128)(2,1)}), (bf16[256,1024]{1,0:T(8,128)(2,1)}, bf16[256,1024]{1,0:T(8,128)(2,1)})) %all-reduce.13.cloned.1.call-update) | async-done | bytes 1048592 | tf_op jit(solution)/shard_map/psum | solution.py:111
  494.1 48.6 %reduce-scatter.11.cloned.1.call-done = bf16[256,1024]{1,0:T(8,128)(2,1)} async-done(((bf16[2048,1024]{1,0:T(8,128)(2,1)}), bf16[256,1024]{1,0:T(8,128)(2,1)}) %reduce-scatter.11.cloned.1.call-update) | async-done | bytes 524304 | tf_op jit(solution)/shard_map/reduce_scatter | solution.py:91
  542.6 54.5 %all-reduce.11.cloned.1.call-done = (bf16[256,1024]{1,0:T(8,128)(2,1)}, bf16[256,1024]{1,0:T(8,128)(2,1)}) async-done(((bf16[256,1024]{1,0:T(8,128)(2,1)}, bf16[256,1024]{1,0:T(8,128)(2,1)}), (bf16[256,1024]{1,0:T(8,128)(2,1)}, bf16[256,1024]{1,0:T(8,128)(2,1)})) %all-reduce.11.cloned.1.call-update) | async-done | bytes 1048592 | tf_op jit(solution)/shard_map/psum | solution.py:111
  601.0 52.9 %all-reduce.9.cloned.1.call-done = (bf16[256,1024]{1,0:T(8,128)(2,1)}, bf16[256,1024]{1,0:T(8,128)(2,1)}) async-done(((bf16[256,1024]{1,0:T(8,128)(2,1)}, bf16[256,1024]{1,0:T(8,128)(2,1)}), (bf16[256,1024]{1,0:T(8,128)(2,1)}, bf16[256,1024]{1,0:T(8,128)(2,1)})) %all-reduce.9.cloned.1.call-update) | async-done | bytes 1048592 | tf_op jit(solution)/shard_map/psum | solution.py:111
  653.9 10.4 %divide_subtract_fusion = (f32[256,4096]{1,0:T(8,128)}, f32[256,4096]{1,0:T(8,128)}, f32[256,4096]{1,0:T(8,128)}) fusion(f32[256,4096]{1,0:T(8,128)} %param.13, bf16[256,1024]{1,0:T(8,128)(2,1)} %get-tuple-element.30, bf16[256,1024]{1,0:T(8,128)(2,1)} %get-tuple-element.16, bf16[256,1024]{1,0:T(8,128)(2,1)} %get-tuple-element.14, ...), kind=kLoop, calls=%fused_computation.12 | loop fusion | flops 36700160 | bytes 29360128 | tf_op jit(solution)/shard_map/sub | solution.py:40
  (43 shorter events, 16.1 us)
Async XLA Ops:
  7.2 63.5 %copy-start = (bf16[512,2048]{1,0:T(8,128)(2,1)S(1)}, bf16[512,2048]{1,0:T(8,128)(2,1)}, u32[]{:S(2)}) copy-start(bf16[512,2048]{1,0:T(8,128)(2,1)} %param.9) | copy-start | bytes 6291460
  7.2 63.4 %all-gather.9.cloned.1.call-start = ((), (), s32[]{:S(2)}) async-start(), calls=%async_computation.6 | async-start | bytes 4718592 | tf_op jit(solution)/shard_map/all_gather | solution.py:72
  20.6 2.3 copy-start.3
  20.6 98.1 %all-gather.5.cloned.1.call-start = ((), (), s32[]{:S(2)}) async-start(), calls=%async_computation.4 | async-start | bytes 4718592 | tf_op jit(solution)/shard_map/all_gather | solution.py:72
  21.4 144.8 %all-gather.11.cloned.1.call-start = ((), (), s32[]{:S(2)}) async-start(), calls=%async_computation.7 | async-start | bytes 4718592 | tf_op jit(solution)/shard_map/all_gather | solution.py:72
  22.1 191.4 %all-gather.7.cloned.1.call-start = ((), (), s32[]{:S(2)}) async-start(), calls=%async_computation.5 | async-start | bytes 4718592 | tf_op jit(solution)/shard_map/all_gather | solution.py:72
  22.7 255.5 %reduce-scatter.7.cloned.1.call-start = ((), (), s32[]{:S(2)}) async-start(), calls=%async_computation.9 | async-start | bytes 4718592 | tf_op jit(solution)/shard_map/reduce_scatter | solution.py:91
  213.6 9.8 %copy-start.4 = (f32[512,1024]{1,0:T(8,128)S(1)}, f32[512,1024]{1,0:T(8,128)}, u32[]{:S(2)}) copy-start(f32[512,1024]{1,0:T(8,128)} %fusion.13) | copy-start | bytes 6291460
  229.3 99.8 %reduce-scatter.5.cloned.1.call-start = ((), (), s32[]{:S(2)}) async-start(), calls=%async_computation.8 | async-start | bytes 4718592 | tf_op jit(solution)/shard_map/reduce_scatter | solution.py:91
  236.0 147.0 %all-reduce.15.cloned.1.call-start = ((), (), s32[]{:S(2)}) async-start(), calls=%async_computation.15 | async-start | bytes 2097152 | tf_op jit(solution)/shard_map/psum | solution.py:111
  282.1 153.8 %reduce-scatter.9.cloned.1.call-start = ((), (), s32[]{:S(2)}) async-start(), calls=%async_computation.10 | async-start | bytes 4718592 | tf_op jit(solution)/shard_map/reduce_scatter | solution.py:91
  288.6 201.3 %all-reduce.13.cloned.1.call-start = ((), (), s32[]{:S(2)}) async-start(), calls=%async_computation.14 | async-start | bytes 2097152 | tf_op jit(solution)/shard_map/psum | solution.py:111
  386.9 155.7 %reduce-scatter.11.cloned.1.call-start = ((), (), s32[]{:S(2)}) async-start(), calls=%async_computation.11 | async-start | bytes 4718592 | tf_op jit(solution)/shard_map/reduce_scatter | solution.py:91
  393.4 203.7 %all-reduce.11.cloned.1.call-start = ((), (), s32[]{:S(2)}) async-start(), calls=%async_computation.13 | async-start | bytes 2097152 | tf_op jit(solution)/shard_map/psum | solution.py:111
  493.7 160.2 %copy-start.1 = (bf16[256,1024]{1,0:T(8,128)(2,1)S(1)}, bf16[256,1024]{1,0:T(8,128)(2,1)}, u32[]{:S(2)}) copy-start(bf16[256,1024]{1,0:T(8,128)(2,1)} %get-tuple-element.12) | copy-start | bytes 1572868
  493.7 160.2 %copy-start.2 = (bf16[256,1024]{1,0:T(8,128)(2,1)S(1)}, bf16[256,1024]{1,0:T(8,128)(2,1)}, u32[]{:S(2)}) copy-start(bf16[256,1024]{1,0:T(8,128)(2,1)} %get-tuple-element.18) | copy-start | bytes 1572868
  493.8 160.2 %all-reduce.9.cloned.1.call-start = ((), (), s32[]{:S(2)}) async-start(), calls=%async_computation.12 | async-start | bytes 2097152 | tf_op jit(solution)/shard_map/psum | solution.py:111
Sparse Core Ops, SparseCore 0:
  20.7 49.8 all-gather.8
  72.8 45.8 all-gather.4
  120.3 45.8 all-gather.10
  167.7 45.8 all-gather.6
  229.4 48.7 reduce-scatter.6
  280.9 48.1 reduce-scatter.4
  332.1 50.8 all-reduce.14
  385.9 50.0 reduce-scatter.8
  439.0 50.8 all-reduce.12
  492.6 50.0 reduce-scatter.10
  546.3 50.8 all-reduce.10
  601.1 52.7 all-reduce.8
where the time goes:
time: 672 us; the launch traced here: 671 us
  waiting for transfers between devices  563 us (84%)
  matrix products  53.4 us (8%)
  other arithmetic  37.2 us (6%)
  between operations  14.9 us (2%)
    psum x4, waiting for transfers between devices, per_device(): sums.append(lax.psum((grad, row_major(curvature)), 'sample'))  215 us
    reduce_scatter x4, waiting for transfers between devices, per_device(): lax.psum_scatter(row_major((lax.dot_general(attn, row_major(back_low), ((...  174 us
    all_gather x4, waiting for transfers between devices, per_device(): lax.all_gather(row_major(sampled), 'fsdp', axis=0, tiled=True)  172 us
    dot_general x4, matrix products, per_device(): jnp.dot(attn, row_major(gathered[c]), preferred_element_type=jnp.float32)  28.2 us
    dot_general x4, matrix products, per_device(): lax.dot_general(attn, row_major(back_low), (((0,), (0,)), ((), ())), pref...  25.2 us
    convert_element_type x4, other arithmetic, per_device(): curvature = (grad.astype(jnp.float32) * epsilons[c]).astype(jnp.bfloat16)  15.5 us
  transfers between devices with their start and end apart: 12, of which 12 were waited for; matrix products, arithmetic and copies ran while one was open for 7% of the time, Pallas kernels for 0%

commit v1 on v0

--- a/solution.py
+++ b/solution.py
@@ -10,6 +10,22 @@
 step_size = 0.3
 damping = 0.1
 norm_eps = 1e-05
+
+
+def collect(x, axis, dim):
+    ways, here, hop = (lax.axis_size(axis), lax.axis_index(axis), x.shape[dim])
+    shape = [n * ways if d == dim else n for d, n in enumerate(x.shape)]
+    full = lax.dynamic_update_slice_in_dim(jnp.zeros(shape, x.dtype), x, here * hop, axis=dim)
+    going_up = going_down = x
+    for far in range(1, ways // 2 + 1):
+        going_up = lax.ppermute(going_up, axis, [(d, (d + 1) % ways) for d in range(ways)])
+        full = lax.dynamic_update_slice_in_dim(full, going_up, (here - far) % ways * hop, axis=dim)
+        if 2 * far < ways:
+            going_down = lax.ppermute(going_down, axis, [(d, (d - 1) % ways) for d in range(ways)])
+            full = lax.dynamic_update_slice_in_dim(
+                full, going_down, (here + far) % ways * hop, axis=dim
+            )
+    return full
 
 
 def noise_table(seed_step, group_id, row_start, row_count, in_width, width, col_start, col_count):
@@ -69,7 +85,7 @@
             + sigma.astype(jnp.bfloat16).astype(jnp.float32) * epsilon
         ).astype(jnp.bfloat16)
         epsilons.append(epsilon / sigma)
-        gathered.append(lax.all_gather(row_major(sampled), "fsdp", axis=0, tiled=True))
+        gathered.append(collect(row_major(sampled), "fsdp", 0))
     totals = []
     square = jnp.zeros((attn.shape[0], 1), jnp.float32)
     cross = jnp.zeros((attn.shape[0], 1), jnp.float32)

time: 672 us -> 635 us (0.945)
  waiting for transfers between devices: 563 us -> 483 us
  starting transfers between devices: 1.15 us -> 40.2 us
  local copies, waits for them, and re-layouts: 1.41 us -> 19.2 us
  matrix products: 53.4 us -> 35.8 us
    all_gather x4 -> x0, waiting for transfers between devices: 172 us -> none  [per_device(): lax.all_gather(row_major(sampled), 'fsdp', axis=0, tiled=True)]
    ppermute x0 -> x28, waiting for transfers between devices: none -> 93.7 us  [the longest x16 84.3 us: collect(): lax.ppermute(going_up, axis, [(d, (d + 1) % ways) for d in range(ways)])]
    ppermute x0 -> x28, starting transfers between devices: none -> 39.4 us  [the longest x12 28.9 us: collect(): lax.ppermute(going_down, axis, [(d, (d - 1) % ways) for d in range(ways)])]
    dot_general x4, matrix products: 28.2 us -> 11.8 us  [per_device(): jnp.dot(attn, row_major(gathered[c]), preferred_element_type=jnp.float32)]
    dynamic_update_slice x0 -> x28, local copies, waits for them, and re-layouts: none -> 12.8 us  [the longest x16 6.93 us: collect(): lax.dynamic_update_slice_in_dim(full, going_up, (here - far) % ways * hop...]
    dynamic_update_slice x0 -> x4, other arithmetic: none -> 9.9 us  [collect(): lax.dynamic_update_slice_in_dim(jnp.zeros(shape, x.dtype), x, here * hop,...]
    convert_element_type x1 -> x0, other arithmetic: 7.5 us -> none  [per_device(): sampled = (mean[:, cut].astype(jnp.bfloat16).astype(jnp.float32) + sigma....]
  transfers between devices with their start and end apart: 12 -> 36, of which waited for: 12 -> 28; matrix products, arithmetic and copies ran while one was open for 7% -> 9% of each run, Pallas kernels for 0% -> 0%
where the time goes in v1:
time: 635 us; the launch traced here: 634 us
  waiting for transfers between devices  483 us (76%)
  starting transfers between devices  40.2 us (6%)
  other arithmetic  40 us (6%)
  matrix products  35.8 us (6%)
  local copies, waits for them, and re-layouts  19.2 us (3%)
  between operations  15.4 us (2%)
    psum x4, waiting for transfers between devices, per_device(): sums.append(lax.psum((grad, row_major(curvature)), 'sample'))  215 us
    reduce_scatter x4, waiting for transfers between devices, per_device(): lax.psum_scatter(row_major((lax.dot_general(attn, row_major(back_low), ((...  174 us
    ppermute x16, waiting for transfers between devices, collect(): lax.ppermute(going_up, axis, [(d, (d + 1) % ways) for d in range(ways)])  84.3 us
    ppermute x12, starting transfers between devices, collect(): lax.ppermute(going_down, axis, [(d, (d - 1) % ways) for d in range(ways)])  28.9 us
    dot_general x4, matrix products, per_device(): lax.dot_general(attn, row_major(back_low), (((0,), (0,)), ((), ())), pref...  23.9 us
    convert_element_type x4, other arithmetic, per_device(): curvature = (grad.astype(jnp.float32) * epsilons[c]).astype(jnp.bfloat16)  15.9 us
  transfers between devices with their start and end apart: 36, of which 28 were waited for; matrix products, arithmetic and copies ran while one was open for 9% of the time, Pallas kernels for 0%

profile of v1, /device:TPU:0, one launch (start us, length us, event | category | flops | bytes accessed | tf_op | source)
XLA Modules:
  0.0 634.1 jit_solution(11276024281326858091)
XLA Ops:
  62.5 4.1 collective-permute-done.7
  72.1 5.7 collective-permute-done.16
  77.9 11.2 %collective-permute-done.2 = bf16[256,1024]{1,0:T(8,128)(2,1)S(1)} collective-permute-done((bf16[256,1024]{1,0:T(8,128)(2,1)}, bf16[256,1024]{1,0:T(8,128)(2,1)S(1)}, u32[]{:S(2)}, u32[]{:S(2)}) %collective-permute-start.2) | collective-permute-done | bytes 524320 | tf_op jit(solution)/shard_map/ppermute | solution.py:21
  95.3 5.0 collective-permute-done.23
  106.6 4.9 collective-permute-done.9
  117.0 5.7 collective-permute-done.18
  122.8 11.2 %collective-permute-done.4 = bf16[256,1024]{1,0:T(8,128)(2,1)S(1)} collective-permute-done((bf16[256,1024]{1,0:T(8,128)(2,1)S(1)}, bf16[256,1024]{1,0:T(8,128)(2,1)S(1)}, u32[]{:S(2)}, u32[]{:S(2)}) %collective-permute-start.4) | collective-permute-done | bytes 524320 | tf_op jit(solution)/shard_map/ppermute | solution.py:21
  139.5 5.7 collective-permute-done.25
  145.3 11.2 %collective-permute-done.11 = bf16[256,1024]{1,0:T(8,128)(2,1)S(1)} collective-permute-done((bf16[256,1024]{1,0:T(8,128)(2,1)S(1)}, bf16[256,1024]{1,0:T(8,128)(2,1)S(1)}, u32[]{:S(2)}, u32[]{:S(2)}) %collective-permute-start.11) | collective-permute-done | bytes 524320 | tf_op jit(solution)/shard_map/ppermute | solution.py:21
  159.1 5.7 collective-permute-done.20
  181.7 4.7 multiply_reduce_fusion.2
  186.4 4.6 fusion.7
  191.4 6.4 %fusion.6 = bf16[2048,1024]{1,0:T(8,128)(2,1)} fusion(bf16[512,2048]{1,0:T(8,128)(2,1)S(1)} %copy-done, f32[512,1024]{1,0:T(8,128)} %get-tuple-element.56, f32[512]{0:T(512)S(1)} %get-tuple-element.40, f32[1024]{0:T(1024)S(1)} %get-tuple-element.52, f32[512]{0:T(512)S(1)} %get-tuple-element.41, bf16[512,4096]{1,0:T(8,128)(2,1)} %param.11), kind=kOutput, calls=%fused_computation.14 | convolution fusion | flops 2154823680 | bytes 9445376 | tf_op jit(solution)/shard_map/dot_general | solution.py:110
  197.9 43.3 %reduce-scatter.7.cloned.1.call-done = bf16[256,1024]{1,0:T(8,128)(2,1)} async-done(((bf16[2048,1024]{1,0:T(8,128)(2,1)}), bf16[256,1024]{1,0:T(8,128)(2,1)}) %reduce-scatter.7.cloned.1.call-update) | async-done | bytes 524304 | tf_op jit(solution)/shard_map/reduce_scatter | solution.py:107
  245.3 6.4 %fusion.8 = bf16[2048,1024]{1,0:T(8,128)(2,1)} fusion(bf16[512,2048]{1,0:T(8,128)(2,1)S(1)} %copy-done, f32[512,1024]{1,0:T(8,128)} %copy-done.17, f32[512]{0:T(512)S(1)} %get-tuple-element.40, f32[1024]{0:T(1024)S(1)} %get-tuple-element.50, f32[512]{0:T(512)S(1)} %get-tuple-element.41, bf16[512,4096]{1,0:T(8,128)(2,1)} %param.11), kind=kOutput, calls=%fused_computation.16 | convolution fusion | flops 2154823680 | bytes 9445376 | tf_op jit(solution)/shard_map/dot_general | solution.py:110
  251.8 40.5 %reduce-scatter.5.cloned.1.call-done = bf16[256,1024]{1,0:T(8,128)(2,1)} async-done(((bf16[2048,1024]{1,0:T(8,128)(2,1)}), bf16[256,1024]{1,0:T(8,128)(2,1)}) %reduce-scatter.5.cloned.1.call-update) | async-done | bytes 524304 | tf_op jit(solution)/shard_map/reduce_scatter | solution.py:107
  292.3 53.9 %all-reduce.15.cloned.1.call-done = (bf16[256,1024]{1,0:T(8,128)(2,1)}, bf16[256,1024]{1,0:T(8,128)(2,1)}) async-done(((bf16[256,1024]{1,0:T(8,128)(2,1)}, bf16[256,1024]{1,0:T(8,128)(2,1)}), (bf16[256,1024]{1,0:T(8,128)(2,1)}, bf16[256,1024]{1,0:T(8,128)(2,1)})) %all-reduce.15.cloned.1.call-update) | async-done | bytes 1048592 | tf_op jit(solution)/shard_map/psum | solution.py:127
  350.2 6.4 %fusion.9 = bf16[2048,1024]{1,0:T(8,128)(2,1)} fusion(bf16[512,2048]{1,0:T(8,128)(2,1)S(1)} %copy-done, f32[512,1024]{1,0:T(8,128)} %copy-done.16, f32[512]{0:T(512)S(1)} %get-tuple-element.40, f32[1024]{0:T(1024)S(1)} %get-tuple-element.53, f32[512]{0:T(512)S(1)} %get-tuple-element.41, bf16[512,4096]{1,0:T(8,128)(2,1)} %param.11), kind=kOutput, calls=%fused_computation.17 | convolution fusion | flops 2154823680 | bytes 9445376 | tf_op jit(solution)/shard_map/dot_general | solution.py:110
  356.8 42.2 %reduce-scatter.9.cloned.1.call-done = bf16[256,1024]{1,0:T(8,128)(2,1)} async-done(((bf16[2048,1024]{1,0:T(8,128)(2,1)}), bf16[256,1024]{1,0:T(8,128)(2,1)}) %reduce-scatter.9.cloned.1.call-update) | async-done | bytes 524304 | tf_op jit(solution)/shard_map/reduce_scatter | solution.py:107
  399.0 53.8 %all-reduce.13.cloned.1.call-done = (bf16[256,1024]{1,0:T(8,128)(2,1)}, bf16[256,1024]{1,0:T(8,128)(2,1)}) async-done(((bf16[256,1024]{1,0:T(8,128)(2,1)}, bf16[256,1024]{1,0:T(8,128)(2,1)}), (bf16[256,1024]{1,0:T(8,128)(2,1)}, bf16[256,1024]{1,0:T(8,128)(2,1)})) %all-reduce.13.cloned.1.call-update) | async-done | bytes 1048592 | tf_op jit(solution)/shard_map/psum | solution.py:127
  457.0 48.5 %reduce-scatter.11.cloned.1.call-done = bf16[256,1024]{1,0:T(8,128)(2,1)} async-done(((bf16[2048,1024]{1,0:T(8,128)(2,1)}), bf16[256,1024]{1,0:T(8,128)(2,1)}) %reduce-scatter.11.cloned.1.call-update) | async-done | bytes 524304 | tf_op jit(solution)/shard_map/reduce_scatter | solution.py:107
  505.5 54.5 %all-reduce.11.cloned.1.call-done = (bf16[256,1024]{1,0:T(8,128)(2,1)}, bf16[256,1024]{1,0:T(8,128)(2,1)}) async-done(((bf16[256,1024]{1,0:T(8,128)(2,1)}, bf16[256,1024]{1,0:T(8,128)(2,1)}), (bf16[256,1024]{1,0:T(8,128)(2,1)}, bf16[256,1024]{1,0:T(8,128)(2,1)})) %all-reduce.11.cloned.1.call-update) | async-done | bytes 1048592 | tf_op jit(solution)/shard_map/psum | solution.py:127
  564.0 52.9 %all-reduce.9.cloned.1.call-done = (bf16[256,1024]{1,0:T(8,128)(2,1)}, bf16[256,1024]{1,0:T(8,128)(2,1)}) async-done(((bf16[256,1024]{1,0:T(8,128)(2,1)}, bf16[256,1024]{1,0:T(8,128)(2,1)}), (bf16[256,1024]{1,0:T(8,128)(2,1)}, bf16[256,1024]{1,0:T(8,128)(2,1)})) %all-reduce.9.cloned.1.call-update) | async-done | bytes 1048592 | tf_op jit(solution)/shard_map/psum | solution.py:127
  616.9 10.4 %divide_subtract_fusion = (f32[256,4096]{1,0:T(8,128)}, f32[256,4096]{1,0:T(8,128)}, f32[256,4096]{1,0:T(8,128)}) fusion(f32[256,4096]{1,0:T(8,128)} %param.13, bf16[256,1024]{1,0:T(8,128)(2,1)} %get-tuple-element.30, bf16[256,1024]{1,0:T(8,128)(2,1)} %get-tuple-element.16, bf16[256,1024]{1,0:T(8,128)(2,1)} %get-tuple-element.14, ...), kind=kLoop, calls=%fused_computation.12 | loop fusion | flops 36700160 | bytes 29360128 | tf_op jit(solution)/shard_map/sub | solution.py:56
  (149 shorter events, 119.7 us)
Async XLA Ops:
  7.2 234.0 %reduce-scatter.7.cloned.1.call-start = ((), (), s32[]{:S(2)}) async-start(), calls=%async_computation.5 | async-start | bytes 4718592 | tf_op jit(solution)/shard_map/reduce_scatter | solution.py:107
  18.8 27.3 %collective-permute-start.15 = (bf16[256,1024]{1,0:T(8,128)(2,1)}, bf16[256,1024]{1,0:T(8,128)(2,1)}, u32[]{:S(2)}, u32[]{:S(2)}) collective-permute-start(bf16[256,1024]{1,0:T(8,128)(2,1)} %get-tuple-element.43), channel_id=1, source_target_pairs={{0,7},{1,0},{2,1},{3,2},{4,3},{5,4},{6,5},{7,6},{8,15},{9,8},{10,9... | collective-permute-start | bytes 1572872 | tf_op jit(solution)/shard_map/ppermute | solution.py:24
  26.0 25.5 %collective-permute-start.1 = (bf16[256,1024]{1,0:T(8,128)(2,1)}, bf16[256,1024]{1,0:T(8,128)(2,1)}, u32[]{:S(2)}, u32[]{:S(2)}) collective-permute-start(bf16[256,1024]{1,0:T(8,128)(2,1)} %get-tuple-element.45), channel_id=1, source_target_pairs={{0,7},{1,0},{2,1},{3,2},{4,3},{5,4},{6,5},{7,6},{8,15},{9,8},{10,9... | collective-permute-start | bytes 1572872 | tf_op jit(solution)/shard_map/ppermute | solution.py:24
  51.5 26.3 %collective-permute-start.16 = (bf16[256,1024]{1,0:T(8,128)(2,1)}, bf16[256,1024]{1,0:T(8,128)(2,1)S(1)}, u32[]{:S(2)}, u32[]{:S(2)}) collective-permute-start(bf16[256,1024]{1,0:T(8,128)(2,1)} %collective-permute-done.14), channel_id=1, source_target_pairs={{0,1},{1,2},{2,3},{3,4},{4,5},{5,6},{6,7},{7,0},{8,9},{9,10},{10,1... | collective-permute-start | bytes 1572872 | tf_op jit(solution)/shard_map/ppermute | solution.py:21
  55.5 33.6 %collective-permute-start.2 = (bf16[256,1024]{1,0:T(8,128)(2,1)}, bf16[256,1024]{1,0:T(8,128)(2,1)S(1)}, u32[]{:S(2)}, u32[]{:S(2)}) collective-permute-start(bf16[256,1024]{1,0:T(8,128)(2,1)} %collective-permute-done), channel_id=1, source_target_pairs={{0,1},{1,2},{2,3},{3,4},{4,5},{5,6},{6,7},{7,0},{8,9},{9,10},{10,1... | collective-permute-start | bytes 1572872 | tf_op jit(solution)/shard_map/ppermute | solution.py:21
  57.9 32.0 %collective-permute-start.17 = (bf16[256,1024]{1,0:T(8,128)(2,1)}, bf16[256,1024]{1,0:T(8,128)(2,1)S(1)}, u32[]{:S(2)}, u32[]{:S(2)}) collective-permute-start(bf16[256,1024]{1,0:T(8,128)(2,1)} %collective-permute-done.15), channel_id=1, source_target_pairs={{0,7},{1,0},{2,1},{3,2},{4,3},{5,4},{6,5},{7,6},{8,15},{9,8},{10,9... | collective-permute-start | bytes 1572872 | tf_op jit(solution)/shard_map/ppermute | solution.py:24
  66.6 26.9 %collective-permute-start.3 = (bf16[256,1024]{1,0:T(8,128)(2,1)}, bf16[256,1024]{1,0:T(8,128)(2,1)S(1)}, u32[]{:S(2)}, u32[]{:S(2)}) collective-permute-start(bf16[256,1024]{1,0:T(8,128)(2,1)} %collective-permute-done.1), channel_id=1, source_target_pairs={{0,7},{1,0},{2,1},{3,2},{4,3},{5,4},{6,5},{7,6},{8,15},{9,8},{10,9... | collective-permute-start | bytes 1572872 | tf_op jit(solution)/shard_map/ppermute | solution.py:24
  69.2 31.1 %collective-permute-start.23 = (bf16[256,1024]{1,0:T(8,128)(2,1)}, bf16[256,1024]{1,0:T(8,128)(2,1)S(1)}, u32[]{:S(2)}, u32[]{:S(2)}) collective-permute-start(bf16[256,1024]{1,0:T(8,128)(2,1)} %collective-permute-done.21), channel_id=1, source_target_pairs={{0,1},{1,2},{2,3},{3,4},{4,5},{5,6},{6,7},{7,0},{8,9},{9,10},{10,1... | collective-permute-start | bytes 1572872 | tf_op jit(solution)/shard_map/ppermute | solution.py:21
  93.5 29.3 %collective-permute-start.18 = (bf16[256,1024]{1,0:T(8,128)(2,1)S(1)}, bf16[256,1024]{1,0:T(8,128)(2,1)S(1)}, u32[]{:S(2)}, u32[]{:S(2)}) collective-permute-start(bf16[256,1024]{1,0:T(8,128)(2,1)S(1)} %collective-permute-done.16), channel_id=1, source_target_pairs={{0,1},{1,2},{2,3},{3,4},{4,5},{5,6},{6,7},{7,0},{8,9},{9,10},{10,1... | collective-permute-start | bytes 1572872 | tf_op jit(solution)/shard_map/ppermute | solution.py:21
  100.3 33.7 %collective-permute-start.4 = (bf16[256,1024]{1,0:T(8,128)(2,1)S(1)}, bf16[256,1024]{1,0:T(8,128)(2,1)S(1)}, u32[]{:S(2)}, u32[]{:S(2)}) collective-permute-start(bf16[256,1024]{1,0:T(8,128)(2,1)S(1)} %collective-permute-done.2), channel_id=1, source_target_pairs={{0,1},{1,2},{2,3},{3,4},{4,5},{5,6},{6,7},{7,0},{8,9},{9,10},{10,1... | collective-permute-start | bytes 1572872 | tf_op jit(solution)/shard_map/ppermute | solution.py:21
  102.9 31.2 %collective-permute-start.19 = (bf16[256,1024]{1,0:T(8,128)(2,1)S(1)}, bf16[256,1024]{1,0:T(8,128)(2,1)S(1)}, u32[]{:S(2)}, u32[]{:S(2)}) collective-permute-start(bf16[256,1024]{1,0:T(8,128)(2,1)S(1)} %collective-permute-done.17), channel_id=1, source_target_pairs={{0,7},{1,0},{2,1},{3,2},{4,3},{5,4},{6,5},{7,6},{8,15},{9,8},{10,9... | collective-permute-start | bytes 1572872 | tf_op jit(solution)/shard_map/ppermute | solution.py:24
  111.5 25.8 %collective-permute-start.5 = (bf16[256,1024]{1,0:T(8,128)(2,1)S(1)}, bf16[256,1024]{1,0:T(8,128)(2,1)S(1)}, u32[]{:S(2)}, u32[]{:S(2)}) collective-permute-start(bf16[256,1024]{1,0:T(8,128)(2,1)S(1)} %collective-permute-done.3), channel_id=1, source_target_pairs={{0,7},{1,0},{2,1},{3,2},{4,3},{5,4},{6,5},{7,6},{8,15},{9,8},{10,9... | collective-permute-start | bytes 1572872 | tf_op jit(solution)/shard_map/ppermute | solution.py:24
  114.1 31.1 %collective-permute-start.25 = (bf16[256,1024]{1,0:T(8,128)(2,1)S(1)}, bf16[256,1024]{1,0:T(8,128)(2,1)S(1)}, u32[]{:S(2)}, u32[]{:S(2)}) collective-permute-start(bf16[256,1024]{1,0:T(8,128)(2,1)S(1)} %collective-permute-done.23), channel_id=1, source_target_pairs={{0,1},{1,2},{2,3},{3,4},{4,5},{5,6},{6,7},{7,0},{8,9},{9,10},{10,1... | collective-permute-start | bytes 1572872 | tf_op jit(solution)/shard_map/ppermute | solution.py:21
  122.8 33.7 %collective-permute-start.11 = (bf16[256,1024]{1,0:T(8,128)(2,1)S(1)}, bf16[256,1024]{1,0:T(8,128)(2,1)S(1)}, u32[]{:S(2)}, u32[]{:S(2)}) collective-permute-start(bf16[256,1024]{1,0:T(8,128)(2,1)S(1)} %collective-permute-done.9), channel_id=1, source_target_pairs={{0,1},{1,2},{2,3},{3,4},{4,5},{5,6},{6,7},{7,0},{8,9},{9,10},{10,1... | collective-permute-start | bytes 1572872 | tf_op jit(solution)/shard_map/ppermute | solution.py:21
  137.4 27.4 %collective-permute-start.20 = (bf16[256,1024]{1,0:T(8,128)(2,1)S(1)}, bf16[256,1024]{1,0:T(8,128)(2,1)S(1)}, u32[]{:S(2)}, u32[]{:S(2)}) collective-permute-start(bf16[256,1024]{1,0:T(8,128)(2,1)S(1)} %collective-permute-done.18), channel_id=1, source_target_pairs={{0,1},{1,2},{2,3},{3,4},{4,5},{5,6},{6,7},{7,0},{8,9},{9,10},{10,1... | collective-permute-start | bytes 1572872 | tf_op jit(solution)/shard_map/ppermute | solution.py:21
  145.2 25.1 %collective-permute-start.6 = (bf16[256,1024]{1,0:T(8,128)(2,1)S(1)}, bf16[256,1024]{1,0:T(8,128)(2,1)S(1)}, u32[]{:S(2)}, u32[]{:S(2)}) collective-permute-start(bf16[256,1024]{1,0:T(8,128)(2,1)S(1)} %collective-permute-done.4), channel_id=1, source_target_pairs={{0,1},{1,2},{2,3},{3,4},{4,5},{5,6},{6,7},{7,0},{8,9},{9,10},{10,1... | collective-permute-start | bytes 1572872 | tf_op jit(solution)/shard_map/ppermute | solution.py:21
  156.5 25.1 %collective-permute-start.13 = (bf16[256,1024]{1,0:T(8,128)(2,1)S(1)}, bf16[256,1024]{1,0:T(8,128)(2,1)S(1)}, u32[]{:S(2)}, u32[]{:S(2)}) collective-permute-start(bf16[256,1024]{1,0:T(8,128)(2,1)S(1)} %collective-permute-done.11), channel_id=1, source_target_pairs={{0,1},{1,2},{2,3},{3,4},{4,5},{5,6},{6,7},{7,0},{8,9},{9,10},{10,1... | collective-permute-start | bytes 1572872 | tf_op jit(solution)/shard_map/ppermute | solution.py:21
  191.1 101.2 %reduce-scatter.5.cloned.1.call-start = ((), (), s32[]{:S(2)}) async-start(), calls=%async_computation.4 | async-start | bytes 4718592 | tf_op jit(solution)/shard_map/reduce_scatter | solution.py:107
  197.8 148.4 %all-reduce.15.cloned.1.call-start = ((), (), s32[]{:S(2)}) async-start(), calls=%async_computation.11 | async-start | bytes 2097152 | tf_op jit(solution)/shard_map/psum | solution.py:127
  245.2 153.7 %reduce-scatter.9.cloned.1.call-start = ((), (), s32[]{:S(2)}) async-start(), calls=%async_computation.6 | async-start | bytes 4718592 | tf_op jit(solution)/shard_map/reduce_scatter | solution.py:107
  251.8 201.0 %all-reduce.13.cloned.1.call-start = ((), (), s32[]{:S(2)}) async-start(), calls=%async_computation.10 | async-start | bytes 2097152 | tf_op jit(solution)/shard_map/psum | solution.py:127
  350.2 155.3 %reduce-scatter.11.cloned.1.call-start = ((), (), s32[]{:S(2)}) async-start(), calls=%async_computation.7 | async-start | bytes 4718592 | tf_op jit(solution)/shard_map/reduce_scatter | solution.py:107
  356.7 203.3 %all-reduce.11.cloned.1.call-start = ((), (), s32[]{:S(2)}) async-start(), calls=%async_computation.9 | async-start | bytes 2097152 | tf_op jit(solution)/shard_map/psum | solution.py:127
  456.7 160.2 %all-reduce.9.cloned.1.call-start = ((), (), s32[]{:S(2)}) async-start(), calls=%async_computation.8 | async-start | bytes 2097152 | tf_op jit(solution)/shard_map/psum | solution.py:127
  (30 other events, 1186.5 us)
Sparse Core Ops, SparseCore 0:
  191.2 49.9 reduce-scatter.6
  244.1 48.1 reduce-scatter.4
  295.3 50.8 all-reduce.14
  348.9 49.9 reduce-scatter.8
  401.9 50.8 all-reduce.12
  455.5 50.0 reduce-scatter.10
  509.1 50.8 all-reduce.10
  564.1 52.7 all-reduce.8
